TPU v7x, 32 devices: a whole 2x2x4 slice. The times are simulated.
32 devices in a mesh: dp: 8 (over z, x), ctx: 4 (over y, core).
Axes of the slice: x: 2, y: 2, z: 4, core: 2. Of those that a mesh axis runs over, the one named last changes fastest.
Arguments:
- hidden_in: bfloat16 [32, 1024, 960], P('dp', 'ctx'), may hold values from -41 to 41
- norm_gains: bfloat16 [1920], P(('dp', 'ctx')), may hold values from 0.099609375 to 1.8984375
- w_query: bfloat16 [960, 960], P('ctx', 'dp'), may hold values from -0.1875 to 0.1875
- w_key: bfloat16 [960, 320], P('ctx', 'dp'), may hold values from -0.1875 to 0.1875
- w_value: bfloat16 [960, 320], P('ctx', 'dp'), may hold values from -0.1875 to 0.1875
- w_out: bfloat16 [960, 960], P('ctx', 'dp'), may hold values from -1.5 to 1.5
- w_gate: bfloat16 [960, 2560], P('ctx', 'dp'), may hold values from -0.1875 to 0.1875
- w_up: bfloat16 [960, 2560], P('ctx', 'dp'), may hold values from -0.1875 to 0.1875
- w_down: bfloat16 [2560, 960], P('ctx', 'dp'), may hold values from -0.125 to 0.125
- cotangent: bfloat16 [32, 1024, 960], P('dp', 'ctx'), may hold values from -6 to 6
Outputs:
- hidden_out: bfloat16 [32, 1024, 960], P('dp', 'ctx')
- hidden_grad: bfloat16 [32, 1024, 960], P('dp', 'ctx')
- gains_grad: float32 [1920], P(('dp', 'ctx'))
- query_grad: float32 [960, 960], P('ctx', 'dp')
- key_grad: float32 [960, 320], P('ctx', 'dp')
- value_grad: float32 [960, 320], P('ctx', 'dp')
- out_grad: float32 [960, 960], P('ctx', 'dp')
- gate_grad: float32 [960, 2560], P('ctx', 'dp')
- up_grad: float32 [960, 2560], P('ctx', 'dp')
- down_grad: float32 [2560, 960], P('ctx', 'dp')
All inputs are finite; a program needn't handle non-finite values.
Results may differ from a plain program's by a relative error of at most 0.014.
Values may be sent and summed in bfloat16 or wider, within the bound.
No kernel may reach another device: no remote copies, remote signals or barrier semaphores. Data moves between devices by JAX's collectives and lax.ppermute only.
A program may use at most 640 MiB of HBM per device.

v0:
```python
import math
import jax
import jax.numpy as jnp
from jax import lax
from jax.sharding import PartitionSpec as P

QH = 15
KVH = 5
HD = 64
epsilon = 1e-05
rope_base = 100000.0
masked_score = -1e30
contract_last = (((1,), (1,)), ((), ()))
contract_first = (((0,), (0,)), ((), ()))


def rope_tables(positions, head_size):
    half_size = head_size // 2
    frequencies = jnp.exp(
        -(jnp.arange(half_size).astype(jnp.float32) * (2.0 / head_size)) * math.log(rope_base)
    )
    angles = positions[:, None] * frequencies[None, :]
    angles = jnp.concatenate([angles, angles], axis=-1)
    return (jnp.cos(angles), jnp.sin(angles))


def rotate(values, cos_table, sin_table):
    half_size = values.shape[-1] // 2
    turned = jnp.concatenate([-values[..., half_size:], values[..., :half_size]], axis=-1)
    return values * cos_table[:, None, :] + turned * sin_table[:, None, :]


def unrotate(grad_turned, cos_table, sin_table):
    primal_out, pullback = jax.vjp(lambda values: rotate(values, cos_table, sin_table), grad_turned)
    return pullback(grad_turned)[0]


def rms_scale(values, gain_row):
    return (
        values * lax.rsqrt(jnp.mean(values * values, axis=-1, keepdims=True) + epsilon) * gain_row
    )


def local(hidden_in, norm_gains, w_query, w_key, w_value, w_out, w_gate, w_up, w_down, cotangent):
    seqs_here, seg_len, model_width = hidden_in.shape
    ctx_size = lax.axis_size("ctx")
    dp_size = lax.axis_size("dp")
    full_len = seg_len * ctx_size
    rows_here = seqs_here * seg_len
    per_group = QH // KVH
    score_scale = HD ** (-0.5)
    row_parts = (
        lax.all_gather(w_query, "ctx", axis=0, tiled=True),
        lax.all_gather(w_key, "ctx", axis=0, tiled=True),
        lax.all_gather(w_value, "ctx", axis=0, tiled=True),
        lax.all_gather(w_out, "ctx", axis=0, tiled=True),
        lax.all_gather(w_gate, "ctx", axis=0, tiled=True),
        lax.all_gather(w_up, "ctx", axis=0, tiled=True),
        lax.all_gather(w_down, "ctx", axis=0, tiled=True),
        lax.all_gather(norm_gains.reshape(-1, 1), "ctx", axis=0, tiled=True),
    )
    gathered = (
        lax.all_gather(row_parts[0], "dp", axis=1, tiled=True),
        lax.all_gather(row_parts[1], "dp", axis=1, tiled=True),
        lax.all_gather(row_parts[2], "dp", axis=1, tiled=True),
        lax.all_gather(row_parts[3], "dp", axis=1, tiled=True),
        lax.all_gather(row_parts[4], "dp", axis=1, tiled=True),
        lax.all_gather(row_parts[5], "dp", axis=1, tiled=True),
        lax.all_gather(row_parts[6], "dp", axis=1, tiled=True),
        lax.all_gather(row_parts[7].reshape(1, -1), "dp", axis=1, tiled=True),
    )
    first_pos = lax.axis_index("ctx") * seg_len + jnp.arange(seg_len)
    cos_table, sin_table = rope_tables(first_pos.astype(jnp.float32), HD)
    row_pos = jnp.tile(first_pos, per_group)
    causal_mask = jnp.arange(full_len)[None, :] <= row_pos[:, None]

    def group_queries(tensor):
        return (
            tensor.reshape(seqs_here, seg_len, KVH, per_group, HD)
            .transpose(0, 2, 3, 1, 4)
            .reshape(seqs_here * KVH, per_group * seg_len, HD)
        )

    def ungroup_queries(tensor):
        return (
            tensor.reshape(seqs_here, KVH, per_group, seg_len, HD)
            .transpose(0, 3, 1, 2, 4)
            .reshape(rows_here, QH * HD)
        )

    def group_keys(tensor):
        return (
            tensor.reshape(seqs_here, full_len, KVH, HD)
            .transpose(0, 2, 1, 3)
            .reshape(seqs_here * KVH, full_len, HD)
        )

    def ungroup_keys(tensor):
        return (
            tensor.reshape(seqs_here, KVH, full_len, HD)
            .transpose(0, 2, 1, 3)
            .reshape(seqs_here, full_len, KVH * HD)
        )

    def block_scores(query_block, key_block):
        raw_scores = (
            lax.dot_general(
                query_block, key_block, contract_last, preferred_element_type=jnp.float32
            )
            * score_scale
        )
        return jnp.where(causal_mask, raw_scores, masked_score)

    def attend_forward(triple):
        query_block, key_block, value_block = triple
        scores = block_scores(query_block, key_block)
        row_top = jnp.max(scores, axis=-1, keepdims=True)
        exponents = jnp.exp(scores - row_top)
        totals = jnp.sum(exponents, axis=-1, keepdims=True)
        attn_weights = exponents / totals
        attended = jnp.dot(
            attn_weights.astype(jnp.bfloat16), value_block, preferred_element_type=jnp.float32
        )
        return (attended, (row_top + jnp.log(totals))[:, 0])

    gains_full = gathered[7].reshape(-1).astype(jnp.float32)
    inputs_f32 = hidden_in.reshape(rows_here, model_width).astype(jnp.float32)
    normed = rms_scale(inputs_f32, gains_full[:model_width]).astype(jnp.bfloat16)
    queries = jnp.dot(normed, gathered[0], preferred_element_type=jnp.float32).reshape(
        seqs_here, seg_len, QH, HD
    )
    key_proj = jnp.dot(normed, gathered[1], preferred_element_type=jnp.float32).reshape(
        seqs_here, seg_len, KVH, HD
    )
    value_proj = (
        jnp.dot(normed, gathered[2], preferred_element_type=jnp.float32)
        .astype(jnp.bfloat16)
        .reshape(seqs_here, seg_len, KVH * HD)
    )
    turned_query = rotate(queries, cos_table, sin_table).astype(jnp.bfloat16)
    turned_key = (
        rotate(key_proj, cos_table, sin_table)
        .astype(jnp.bfloat16)
        .reshape(seqs_here, seg_len, KVH * HD)
    )
    key_sets = (
        lax.all_gather(turned_key, "ctx", axis=1, tiled=True),
        lax.all_gather(value_proj, "ctx", axis=1, tiled=True),
    )
    grouped_query = group_queries(turned_query)
    attended, log_totals = lax.map(
        attend_forward, (grouped_query, group_keys(key_sets[0]), group_keys(key_sets[1]))
    )
    mixed_heads = ungroup_queries(attended).astype(jnp.bfloat16)
    middle = inputs_f32 + jnp.dot(mixed_heads, gathered[3], preferred_element_type=jnp.float32)
    normed_two = rms_scale(middle, gains_full[model_width:]).astype(jnp.bfloat16)
    gate_pre = jnp.dot(normed_two, gathered[4], preferred_element_type=jnp.float32)
    up_pre = jnp.dot(normed_two, gathered[5], preferred_element_type=jnp.float32)
    product = (jax.nn.silu(gate_pre) * up_pre).astype(jnp.bfloat16)
    result = middle + jnp.dot(product, gathered[6], preferred_element_type=jnp.float32)
    hidden_out = result.astype(jnp.bfloat16).reshape(seqs_here, seg_len, model_width)
    rows_again = (
        lax.all_gather(w_query, "ctx", axis=0, tiled=True),
        lax.all_gather(w_key, "ctx", axis=0, tiled=True),
        lax.all_gather(w_value, "ctx", axis=0, tiled=True),
        lax.all_gather(w_out, "ctx", axis=0, tiled=True),
        lax.all_gather(w_gate, "ctx", axis=0, tiled=True),
        lax.all_gather(w_up, "ctx", axis=0, tiled=True),
        lax.all_gather(w_down, "ctx", axis=0, tiled=True),
        lax.all_gather(norm_gains.reshape(-1, 1), "ctx", axis=0, tiled=True),
    )
    refetched = (
        lax.all_gather(rows_again[0], "dp", axis=1, tiled=True),
        lax.all_gather(rows_again[1], "dp", axis=1, tiled=True),
        lax.all_gather(rows_again[2], "dp", axis=1, tiled=True),
        lax.all_gather(rows_again[3], "dp", axis=1, tiled=True),
        lax.all_gather(rows_again[4], "dp", axis=1, tiled=True),
        lax.all_gather(rows_again[5], "dp", axis=1, tiled=True),
        lax.all_gather(rows_again[6], "dp", axis=1, tiled=True),
        lax.all_gather(rows_again[7].reshape(1, -1), "dp", axis=1, tiled=True),
    )
    keys_again = (
        lax.all_gather(turned_key, "ctx", axis=1, tiled=True),
        lax.all_gather(value_proj, "ctx", axis=1, tiled=True),
    )
    gains_back = refetched[7].reshape(-1).astype(jnp.float32)
    seed_low = cotangent.reshape(rows_here, model_width)
    seed_high = seed_low.astype(jnp.float32)
    down_part = lax.dot_general(
        product, seed_low, contract_first, preferred_element_type=jnp.float32
    )
    grad_product = lax.dot_general(
        seed_low, refetched[6], contract_last, preferred_element_type=jnp.float32
    )
    primal_gate, gate_pull = jax.vjp(
        lambda gate_in, up_in: jax.nn.silu(gate_in) * up_in, gate_pre, up_pre
    )
    grad_gate, grad_up = gate_pull(grad_product)
    grad_gate = grad_gate.astype(jnp.bfloat16)
    grad_up = grad_up.astype(jnp.bfloat16)
    gate_part = lax.dot_general(
        normed_two, grad_gate, contract_first, preferred_element_type=jnp.float32
    )
    up_part = lax.dot_general(
        normed_two, grad_up, contract_first, preferred_element_type=jnp.float32
    )
    grad_normed_two = lax.dot_general(
        grad_gate, refetched[4], contract_last, preferred_element_type=jnp.float32
    ) + lax.dot_general(grad_up, refetched[5], contract_last, preferred_element_type=jnp.float32)
    primal_two, second_pull = jax.vjp(rms_scale, middle, gains_back[model_width:])
    grad_middle_norm, gain_two_part = second_pull(grad_normed_two)
    grad_middle = seed_high + grad_middle_norm
    grad_branch = grad_middle.astype(jnp.bfloat16)
    out_part = lax.dot_general(
        mixed_heads, grad_branch, contract_first, preferred_element_type=jnp.float32
    )
    grad_mixed = lax.dot_general(
        grad_branch, refetched[3], contract_last, preferred_element_type=jnp.float32
    ).astype(jnp.bfloat16)

    def attend_backward(bundle):
        query_block, key_block, value_block, log_total, grad_block = bundle
        scores = block_scores(query_block, key_block)
        attn_weights = jnp.exp(scores - log_total[:, None])
        grad_weights = lax.dot_general(
            grad_block, value_block, contract_last, preferred_element_type=jnp.float32
        )
        grad_values = lax.dot_general(
            attn_weights.astype(jnp.bfloat16),
            grad_block,
            contract_first,
            preferred_element_type=jnp.float32,
        )
        grad_scores = (
            attn_weights
            * (grad_weights - jnp.sum(attn_weights * grad_weights, axis=-1, keepdims=True))
        ).astype(jnp.bfloat16)
        grad_queries = (
            jnp.dot(grad_scores, key_block, preferred_element_type=jnp.float32) * score_scale
        )
        grad_keys = (
            lax.dot_general(
                grad_scores, query_block, contract_first, preferred_element_type=jnp.float32
            )
            * score_scale
        )
        return (grad_queries, grad_keys, grad_values)

    grad_grouped = group_queries(grad_mixed.reshape(seqs_here, seg_len, QH, HD))
    query_blocks, key_blocks, value_blocks = lax.map(
        attend_backward,
        (
            grouped_query,
            group_keys(keys_again[0]),
            group_keys(keys_again[1]),
            log_totals,
            grad_grouped,
        ),
    )
    key_sums = (
        lax.psum_scatter(ungroup_keys(key_blocks), "ctx", scatter_dimension=1, tiled=True),
        lax.psum_scatter(ungroup_keys(value_blocks), "ctx", scatter_dimension=1, tiled=True),
    )
    grad_query = (
        unrotate(
            ungroup_queries(query_blocks).reshape(seqs_here, seg_len, QH, HD), cos_table, sin_table
        )
        .astype(jnp.bfloat16)
        .reshape(rows_here, QH * HD)
    )
    grad_key = (
        unrotate(key_sums[0].reshape(seqs_here, seg_len, KVH, HD), cos_table, sin_table)
        .astype(jnp.bfloat16)
        .reshape(rows_here, KVH * HD)
    )
    grad_value = key_sums[1].astype(jnp.bfloat16).reshape(rows_here, KVH * HD)
    query_part = lax.dot_general(
        normed, grad_query, contract_first, preferred_element_type=jnp.float32
    )
    key_part = lax.dot_general(normed, grad_key, contract_first, preferred_element_type=jnp.float32)
    value_part = lax.dot_general(
        normed, grad_value, contract_first, preferred_element_type=jnp.float32
    )
    grad_normed = (
        lax.dot_general(grad_query, refetched[0], contract_last, preferred_element_type=jnp.float32)
        + lax.dot_general(grad_key, refetched[1], contract_last, preferred_element_type=jnp.float32)
        + lax.dot_general(
            grad_value, refetched[2], contract_last, preferred_element_type=jnp.float32
        )
    )
    primal_one, first_pull = jax.vjp(rms_scale, inputs_f32, gains_back[:model_width])
    grad_inputs_norm, gain_one_part = first_pull(grad_normed)
    hidden_grad = (
        (grad_middle + grad_inputs_norm)
        .astype(jnp.bfloat16)
        .reshape(seqs_here, seg_len, model_width)
    )
    gain_part = jnp.concatenate([gain_one_part, gain_two_part])
    col_sums = (
        lax.psum_scatter(query_part, "dp", scatter_dimension=1, tiled=True),
        lax.psum_scatter(key_part, "dp", scatter_dimension=1, tiled=True),
        lax.psum_scatter(value_part, "dp", scatter_dimension=1, tiled=True),
        lax.psum_scatter(out_part, "dp", scatter_dimension=1, tiled=True),
        lax.psum_scatter(gate_part, "dp", scatter_dimension=1, tiled=True),
        lax.psum_scatter(up_part, "dp", scatter_dimension=1, tiled=True),
        lax.psum_scatter(down_part, "dp", scatter_dimension=1, tiled=True),
        lax.psum_scatter(gain_part.reshape(1, -1), "dp", scatter_dimension=1, tiled=True),
    )
    owned = (
        lax.psum_scatter(col_sums[0], "ctx", scatter_dimension=0, tiled=True),
        lax.psum_scatter(col_sums[1], "ctx", scatter_dimension=0, tiled=True),
        lax.psum_scatter(col_sums[2], "ctx", scatter_dimension=0, tiled=True),
        lax.psum_scatter(col_sums[3], "ctx", scatter_dimension=0, tiled=True),
        lax.psum_scatter(col_sums[4], "ctx", scatter_dimension=0, tiled=True),
        lax.psum_scatter(col_sums[5], "ctx", scatter_dimension=0, tiled=True),
        lax.psum_scatter(col_sums[6], "ctx", scatter_dimension=0, tiled=True),
        lax.psum_scatter(col_sums[7].reshape(-1, 1), "ctx", scatter_dimension=0, tiled=True),
    )
    factor = 1.0 / math.sqrt(dp_size * seqs_here * full_len)
    return (
        hidden_out,
        hidden_grad,
        owned[7].reshape(-1) * factor,
        owned[0] * factor,
        owned[1] * factor,
        owned[2] * factor,
        owned[3] * factor,
        owned[4] * factor,
        owned[5] * factor,
        owned[6] * factor,
    )


def solution(mesh):
    in_specs = (
        P("dp", "ctx", None),
        P(("dp", "ctx")),
        P("ctx", "dp"),
        P("ctx", "dp"),
        P("ctx", "dp"),
        P("ctx", "dp"),
        P("ctx", "dp"),
        P("ctx", "dp"),
        P("ctx", "dp"),
        P("dp", "ctx", None),
    )
    out_specs = (
        P("dp", "ctx", None),
        P("dp", "ctx", None),
        P(("dp", "ctx")),
        P("ctx", "dp"),
        P("ctx", "dp"),
        P("ctx", "dp"),
        P("ctx", "dp"),
        P("ctx", "dp"),
        P("ctx", "dp"),
        P("ctx", "dp"),
    )
    return jax.shard_map(local, mesh=mesh, in_specs=in_specs, out_specs=out_specs, check_vma=False)
```

profile of v0, /device:TPU:0, one launch (start us, length us, event | category | flops | bytes accessed | tf_op | source)
XLA Modules:
  0.0 2127.9 jit_solution(17298331334786552677)
XLA Ops:
  27.9 21.9 %all-reduce.5 = bf16[1920]{0:T(1024)(128)(2,1)S(1)} all-reduce(bf16[1920]{0:T(1024)(128)(2,1)S(1)} %dynamic-update-slice.1), channel_id=3, replica_groups=mesh['dp'=8,'ctx'=4] {'dp'}, use_global_device_ids=true, to_apply=%add.5 | all-reduce | flops 1920 | bytes 7680
  57.8 32.5 %all_gather.77 = bf16[960,320]{0,1:T(8,128)(2,1)S(1)} all-gather(bf16[960,40]{0,1:T(8,128)(2,1)S(1)} %reshape.345), channel_id=1, replica_groups=mesh['dp'=8,'ctx'=4] {'dp'}, dimensions={1}, use_global_device_ids=true | all-gather | bytes 691200 | tf_op jit(solution)/shard_map/all_gather | solution.py:64
  99.0 31.6 %all_gather.80 = bf16[960,320]{0,1:T(8,128)(2,1)S(1)} all-gather(bf16[960,40]{0,1:T(8,128)(2,1)S(1)} %reshape.347), channel_id=1, replica_groups=mesh['dp'=8,'ctx'=4] {'dp'}, dimensions={1}, use_global_device_ids=true | all-gather | bytes 691200 | tf_op jit(solution)/shard_map/all_gather | solution.py:65
  213.6 112.1 %while.30 = (s32[]{:T(128)}, bf16[20,768,64]{1,2,0:T(8,128)(2,1)S(1)}, f32[20,768]{1,0:T(8,128)S(1)}, bf16[20,768,64]{2,1,0:T(8,128)(2,1)}, bf16[20,1024,64]{2,1...) while((s32[]{:T(128)}, bf16[20,768,64]{1,2,0:T(8,128)(2,1)S(1)}, ...), condition=%wide.region_4.5_spmd.clone.clone, body=%wide.region_1.4_spmd.clone.sunk.clone | while | flops 213122304 | bytes 10405977 | solution.py:151
  354.9 31.6 %all-gather.22.cloned.1.call-done = bf16[960,2560]{0,1:T(8,128)(2,1)} async-done(((bf16[960,320]{0,1:T(8,128)(2,1)}), bf16[960,2560]{0,1:T(8,128)(2,1)}) %all-gather.22.cloned.1.call-update) | async-done | bytes 4915216 | tf_op jit(solution)/shard_map/all_gather | solution.py:67
  397.5 71.2 %all-gather.26.cloned.1.call-done = bf16[2560,960]{0,1:T(8,128)(2,1)} async-done(((bf16[2560,120]{0,1:T(8,128)(2,1)}), bf16[2560,960]{0,1:T(8,128)(2,1)}) %all-gather.26.cloned.1.call-update) | async-done | bytes 4915216 | tf_op jit(solution)/shard_map/all_gather | solution.py:69
  468.7 19.1 multiply_convert_fusion.1
  523.7 220.1 %while.31 = (s32[]{:T(128)}, f32[20,768,64]{1,2,0:T(8,128)}, f32[20,1024,64]{1,2,0:T(8,128)}, f32[20,1024,64]{1,2,0:T(8,128)}, bf16[20,768,64]{2,1,0:T(8,128)(2,...) while((s32[]{:T(128)}, f32[20,768,64]{1,2,0:T(8,128)}, ...), condition=%wide.region_9.10_spmd.clone.clone, body=%wide.region_7.9_spmd.clone.sunk.clone | while | flops 511294720 | bytes 25910384 | solution.py:250
  752.8 77.3 %copy.93 = f32[4,1024,320]{0,2,1:T(8,128)} copy(f32[4,1024,320]{1,0,2:T(4,128)} %bitcast.269) | data formatting | bytes 10485760
  830.1 144.6 %reshape.360 = f32[1024,1280]{1,0:T(8,128)} reshape(f32[1024,320,4]{2,1,0:T(8,128)} %bitcast.50) | data formatting | bytes 10485760
  1024.3 47.0 %reshape.361 = bf16[256,320,4]{2,1,0:T(8,128)(2,1)} reshape(f32[256,1280]{1,0:T(8,128)} %reduce-scatter.53.cloned.1.call-done) | data formatting | bytes 1966080
  1071.3 18.7 copy.94
  1135.9 64.6 %reduce-scatter.57.cloned.1.call-done = f32[120,960]{1,0:T(8,128)} async-done(((f32[960,960]{1,0:T(8,128)}), f32[120,960]{1,0:T(8,128)}) %reduce-scatter.57.cloned.1.call-update) | async-done | bytes 460816
  1211.5 56.8 %reduce-scatter.39.cloned.1.call-done = f32[960,40]{0,1:T(8,128)} async-done(((f32[960,320]{0,1:T(8,128)}), f32[960,40]{0,1:T(8,128)}) %reduce-scatter.39.cloned.1.call-update) | async-done | bytes 153616 | tf_op jit(solution)/shard_map/reduce_scatter | solution.py:301
  1270.3 65.4 %reduce-scatter.41.cloned.1.call-done = f32[960,40]{0,1:T(8,128)} async-done(((f32[960,320]{0,1:T(8,128)}), f32[960,40]{0,1:T(8,128)}) %reduce-scatter.41.cloned.1.call-update) | async-done | bytes 153616 | tf_op jit(solution)/shard_map/reduce_scatter | solution.py:302
  1337.7 178.7 %reduce-scatter.47.cloned.1.call-done = f32[960,320]{0,1:T(8,128)} async-done(((f32[960,2560]{0,1:T(8,128)}), f32[960,320]{0,1:T(8,128)}) %reduce-scatter.47.cloned.1.call-update) | async-done | bytes 1228816 | tf_op jit(solution)/shard_map/reduce_scatter | solution.py:305
  1519.3 177.8 %reduce-scatter.45.cloned.1.call-done = f32[960,320]{0,1:T(8,128)} async-done(((f32[960,2560]{0,1:T(8,128)}), f32[960,320]{0,1:T(8,128)}) %reduce-scatter.45.cloned.1.call-update) | async-done | bytes 1228816 | tf_op jit(solution)/shard_map/reduce_scatter | solution.py:304
  1700.8 168.6 %reduce-scatter.49.cloned.1.call-done = f32[2560,120]{0,1:T(8,128)} async-done(((f32[2560,960]{0,1:T(8,128)}), f32[2560,120]{0,1:T(8,128)}) %reduce-scatter.49.cloned.1.call-update) | async-done | bytes 1228816 | tf_op jit(solution)/shard_map/reduce_scatter | solution.py:306
  1893.8 22.8 %reduce-scatter.37.cloned.1.call-done = f32[240,120]{1,0:T(8,128)} async-done(((f32[960,120]{1,0:T(8,128)}), f32[240,120]{1,0:T(8,128)}) %reduce-scatter.37.cloned.1.call-update) | async-done | bytes 115216 | tf_op jit(solution)/shard_map/reduce_scatter | solution.py:310
  1925.0 59.1 %reduce-scatter.55.cloned.1.call-done = f32[240,1]{1,0:T(8,128)} async-done(((f32[1920,1]{1,0:T(8,128)}), f32[240,1]{1,0:T(8,128)}) %reduce-scatter.55.cloned.1.call-update) | async-done | bytes 976
  2007.7 23.0 %reduce-scatter.61.cloned.1.call-done = f32[240,40]{1,0:T(8,128)} async-done(((f32[960,40]{1,0:T(8,128)}), f32[240,40]{1,0:T(8,128)}) %reduce-scatter.61.cloned.1.call-update) | async-done | bytes 38416
  2032.9 27.8 %reduce-scatter.67.cloned.1.call-done = f32[240,320]{1,0:T(8,128)} async-done(((f32[960,320]{1,0:T(8,128)}), f32[240,320]{1,0:T(8,128)}) %reduce-scatter.67.cloned.1.call-update) | async-done | bytes 307216
  2061.8 28.9 %reduce-scatter.65.cloned.1.call-done = f32[240,320]{1,0:T(8,128)} async-done(((f32[960,320]{1,0:T(8,128)}), f32[240,320]{1,0:T(8,128)}) %reduce-scatter.65.cloned.1.call-update) | async-done | bytes 307216
  2093.4 25.7 %reduce-scatter.51.cloned.1.call-done = f32[640,120]{0,1:T(8,128)} async-done(((f32[2560,120]{0,1:T(8,128)}), f32[640,120]{0,1:T(8,128)}) %reduce-scatter.51.cloned.1.call-update) | async-done | bytes 307216 | tf_op jit(solution)/shard_map/reduce_scatter | solution.py:316
  (539 shorter events, 714.5 us)
Async XLA Ops:
  7.2 170.4 %all-gather.14.cloned.1.call-start = ((), (), s32[]{:S(2)}) async-start(), calls=%async_computation.17 | async-start | bytes 2211840 | tf_op jit(solution)/shard_map/all_gather | solution.py:63
  15.6 170.9 %all-gather.16.cloned.1.call-start = ((), (), s32[]{:S(2)}) async-start(), calls=%async_computation.18 | async-start | bytes 3276800 | tf_op jit(solution)/shard_map/all_gather | solution.py:147
  92.5 103.6 %all-gather.18.cloned.1.call-start = ((), (), s32[]{:S(2)}) async-start(), calls=%async_computation.19 | async-start | bytes 3276800 | tf_op jit(solution)/shard_map/all_gather | solution.py:148
  133.9 200.8 %all-gather.20.cloned.1.call-start = ((), (), s32[]{:S(2)}) async-start(), calls=%async_computation.20 | async-start | bytes 2211840 | tf_op jit(solution)/shard_map/all_gather | solution.py:66
  140.5 202.1 %all-gather.24.cloned.1.call-start = ((), (), s32[]{:S(2)}) async-start(), calls=%async_computation.22 | async-start | bytes 5898240 | tf_op jit(solution)/shard_map/all_gather | solution.py:68
  154.5 232.0 %all-gather.22.cloned.1.call-start = ((), (), s32[]{:S(2)}) async-start(), calls=%async_computation.21 | async-start | bytes 5898240 | tf_op jit(solution)/shard_map/all_gather | solution.py:67
  164.5 304.2 %all-gather.26.cloned.1.call-start = ((), (), s32[]{:S(2)}) async-start(), calls=%async_computation.23 | async-start | bytes 5529600 | tf_op jit(solution)/shard_map/all_gather | solution.py:69
  172.8 834.5 %reduce-scatter.35.cloned.1.call-start = ((), (), s32[]{:S(2)}) async-start(), calls=%async_computation.24 | async-start | bytes 6553600 | tf_op jit(solution)/shard_map/reduce_scatter | solution.py:261
  743.8 280.4 %reduce-scatter.53.cloned.1.call-start = ((), (), s32[]{:S(2)}) async-start(), calls=%async_computation.33 | async-start | bytes 6553600
  974.7 152.6 %reduce-scatter.63.cloned.1.call-start = ((), (), s32[]{:S(2)}) async-start(), calls=%async_computation.38 | async-start | bytes 4423680
  983.2 217.3 %reduce-scatter.57.cloned.1.call-start = ((), (), s32[]{:S(2)}) async-start(), calls=%async_computation.35 | async-start | bytes 4423680
  1007.2 261.1 %reduce-scatter.39.cloned.1.call-start = ((), (), s32[]{:S(2)}) async-start(), calls=%async_computation.26 | async-start | bytes 1474560 | tf_op jit(solution)/shard_map/reduce_scatter | solution.py:301
  1012.6 323.2 %reduce-scatter.41.cloned.1.call-start = ((), (), s32[]{:S(2)}) async-start(), calls=%async_computation.27 | async-start | bytes 1474560 | tf_op jit(solution)/shard_map/reduce_scatter | solution.py:302
  1092.1 424.3 %reduce-scatter.47.cloned.1.call-start = ((), (), s32[]{:S(2)}) async-start(), calls=%async_computation.30 | async-start | bytes 11796480 | tf_op jit(solution)/shard_map/reduce_scatter | solution.py:305
  1103.0 594.1 %reduce-scatter.45.cloned.1.call-start = ((), (), s32[]{:S(2)}) async-start(), calls=%async_computation.29 | async-start | bytes 11796480 | tf_op jit(solution)/shard_map/reduce_scatter | solution.py:304
  1115.5 754.0 %reduce-scatter.49.cloned.1.call-start = ((), (), s32[]{:S(2)}) async-start(), calls=%async_computation.31 | async-start | bytes 11059200 | tf_op jit(solution)/shard_map/reduce_scatter | solution.py:306
  1127.2 765.1 %reduce-scatter.43.cloned.1.call-start = ((), (), s32[]{:S(2)}) async-start(), calls=%async_computation.28 | async-start | bytes 614400 | tf_op jit(solution)/shard_map/reduce_scatter | solution.py:313
  1129.4 787.3 %reduce-scatter.37.cloned.1.call-start = ((), (), s32[]{:S(2)}) async-start(), calls=%async_computation.25 | async-start | bytes 614400 | tf_op jit(solution)/shard_map/reduce_scatter | solution.py:310
  1202.5 781.5 %reduce-scatter.55.cloned.1.call-start = ((), (), s32[]{:S(2)}) async-start(), calls=%async_computation.34 | async-start | bytes 1105920
  1211.5 795.3 %reduce-scatter.59.cloned.1.call-start = ((), (), s32[]{:S(2)}) async-start(), calls=%async_computation.36 | async-start | bytes 614400
  1270.3 760.4 %reduce-scatter.61.cloned.1.call-start = ((), (), s32[]{:S(2)}) async-start(), calls=%async_computation.37 | async-start | bytes 614400
  1337.6 723.1 %reduce-scatter.67.cloned.1.call-start = ((), (), s32[]{:S(2)}) async-start(), calls=%async_computation.40 | async-start | bytes 1843200
  1519.3 571.4 %reduce-scatter.65.cloned.1.call-start = ((), (), s32[]{:S(2)}) async-start(), calls=%async_computation.39 | async-start | bytes 1843200
  1700.1 419.0 %reduce-scatter.51.cloned.1.call-start = ((), (), s32[]{:S(2)}) async-start(), calls=%async_computation.32 | async-start | bytes 1536000 | tf_op jit(solution)/shard_map/reduce_scatter | solution.py:316
  (44 other events, 1003.3 us)
Sparse Core Ops, SparseCore 0:
  15.7 49.7 all-gather.13
  92.6 22.4 all-gather.15
  134.0 25.9 all-gather.17
  162.6 51.0 all-gather.19
  215.7 84.5 all-gather.23
  302.4 84.0 all-gather.21
  388.7 79.9 all-gather.25
  744.0 49.4 reduce-scatter.34
  974.8 49.4 reduce-scatter.52
  1027.8 84.6 reduce-scatter.62
  1116.1 84.2 reduce-scatter.56
  1203.7 64.6 reduce-scatter.38
  1271.7 63.9 reduce-scatter.40
  1339.2 177.1 reduce-scatter.46
  1519.8 177.3 reduce-scatter.44
  1700.6 168.7 reduce-scatter.48
  1871.8 20.3 reduce-scatter.42
  1895.2 21.3 reduce-scatter.36
  1920.0 64.0 reduce-scatter.54
  1986.4 20.2 reduce-scatter.58
  2009.3 21.3 reduce-scatter.60
  2033.3 27.3 reduce-scatter.66
  2063.3 27.3 reduce-scatter.64
  2093.2 25.9 reduce-scatter.50
where the time goes:
time: 2140 us; the launch traced here: 2130 us
  waiting for transfers between devices  1040 us (49%)
  matrix products  447 us (21%)
  local copies, waits for them, and re-layouts  414 us (19%)
  blocking collectives  151 us (7%)
  other arithmetic  53.6 us (3%)
    unnamed x127, local copies, waits for them, and re-layouts  346 us
    unnamed x32, waiting for transfers between devices  230 us
    reduce_scatter x1, waiting for transfers between devices, local(): lax.psum_scatter(up_part, 'dp', scatter_dimension=1, tiled=True)  179 us
    reduce_scatter x1, waiting for transfers between devices, local(): lax.psum_scatter(gate_part, 'dp', scatter_dimension=1, tiled=True)  178 us
    reduce_scatter x1, waiting for transfers between devices, local(): lax.psum_scatter(down_part, 'dp', scatter_dimension=1, tiled=True)  169 us
    dot_general x40, matrix products, block_scores(): lax.dot_general(query_block, key_block, contract_last, preferred_element_...  88.5 us
    all_gather x1, waiting for transfers between devices, local(): lax.all_gather(row_parts[6], 'dp', axis=1, tiled=True)  71.2 us
    reduce_scatter x1, waiting for transfers between devices, local(): lax.psum_scatter(value_part, 'dp', scatter_dimension=1, tiled=True)  65.4 us
  transfers between devices with their start and end apart: 24, of which 17 were waited for; matrix products, arithmetic and copies ran while one was open for 29% of the time, Pallas kernels for 0%

commit v1 on v0

--- a/solution.py
+++ b/solution.py
@@ -12,6 +12,18 @@
 masked_score = -1e30
 contract_last = (((1,), (1,)), ((), ()))
 contract_first = (((0,), (0,)), ((), ()))
+
+
+def gather_by_bits(shard, axis, dim):
+    ways, here, step = (lax.axis_size(axis), lax.axis_index(axis), shard.shape[dim])
+    line, have = (shard, 1)
+    while have < ways:
+        line = jnp.concatenate(
+            [line, lax.ppermute(line, axis, [(d, (d - have) % ways) for d in range(ways)])],
+            axis=dim,
+        )
+        have = 2 * have
+    return jnp.roll(line, here * step, axis=dim)
 
 
 def rope_tables(positions, head_size):
@@ -66,7 +78,7 @@
         lax.all_gather(row_parts[3], "dp", axis=1, tiled=True),
         lax.all_gather(row_parts[4], "dp", axis=1, tiled=True),
         lax.all_gather(row_parts[5], "dp", axis=1, tiled=True),
-        lax.all_gather(row_parts[6], "dp", axis=1, tiled=True),
+        gather_by_bits(row_parts[6], "dp", 1),
         lax.all_gather(row_parts[7].reshape(1, -1), "dp", axis=1, tiled=True),
     )
     first_pos = lax.axis_index("ctx") * seg_len + jnp.arange(seg_len)

time: 2140 us -> 2270 us (1.061)
  waiting for transfers between devices: 1040 us -> 1150 us
    reduce_scatter x1, waiting for transfers between devices: 178 us -> 264 us  [local(): lax.psum_scatter(gate_part, 'dp', scatter_dimension=1, tiled=True)]
    ppermute x0 -> x3, waiting for transfers between devices: none -> 24.9 us  [gather_by_bits(): lax.ppermute(line, axis, [(d, (d - have) % ways) for d in range(ways)])]
    unnamed x127 -> x138, local copies, waits for them, and re-layouts: 346 us -> 356 us
  transfers between devices with their start and end apart: 24 -> 27, of which waited for: 17 -> 18; matrix products, arithmetic and copies ran while one was open for 29% -> 28% of each run, Pallas kernels for 0% -> 0%
where the time goes in v1:
time: 2270 us; the launch traced here: 2260 us
  waiting for transfers between devices  1150 us (51%)
  matrix products  448 us (20%)
  local copies, waits for them, and re-layouts  427 us (19%)
  blocking collectives  151 us (7%)
  other arithmetic  56.4 us (2%)
    unnamed x138, local copies, waits for them, and re-layouts  356 us
    reduce_scatter x1, waiting for transfers between devices, local(): lax.psum_scatter(gate_part, 'dp', scatter_dimension=1, tiled=True)  264 us
    unnamed x32, waiting for transfers between devices  237 us
    reduce_scatter x1, waiting for transfers between devices, local(): lax.psum_scatter(up_part, 'dp', scatter_dimension=1, tiled=True)  179 us
    reduce_scatter x1, waiting for transfers between devices, local(): lax.psum_scatter(down_part, 'dp', scatter_dimension=1, tiled=True)  158 us
    dot_general x40, matrix products, block_scores(): lax.dot_general(query_block, key_block, contract_last, preferred_element_...  88.5 us
    all_gather x1, waiting for transfers between devices, local(): lax.all_gather(rows_again[6], 'dp', axis=1, tiled=True)  71.2 us
    reduce_scatter x1, waiting for transfers between devices, local(): lax.psum_scatter(value_part, 'dp', scatter_dimension=1, tiled=True)  65.4 us
  transfers between devices with their start and end apart: 27, of which 18 were waited for; matrix products, arithmetic and copies ran while one was open for 28% of the time, Pallas kernels for 0%

profile of v1, /device:TPU:0, one launch (start us, length us, event | category | flops | bytes accessed | tf_op | source)
XLA Modules:
  0.0 2257.0 jit_solution(8277329817795659173)
XLA Ops:
  27.9 21.9 all-reduce.5
  57.8 32.5 %all_gather.76 = bf16[960,320]{0,1:T(8,128)(2,1)S(1)} all-gather(bf16[960,40]{0,1:T(8,128)(2,1)S(1)} %reshape.345), channel_id=1, replica_groups=mesh['dp'=8,'ctx'=4] {'dp'}, dimensions={1}, use_global_device_ids=true | all-gather | bytes 691200 | tf_op jit(solution)/shard_map/all_gather | solution.py:76
  99.1 31.7 %all_gather.79 = bf16[960,320]{0,1:T(8,128)(2,1)S(1)} all-gather(bf16[960,40]{0,1:T(8,128)(2,1)S(1)} %reshape.347), channel_id=1, replica_groups=mesh['dp'=8,'ctx'=4] {'dp'}, dimensions={1}, use_global_device_ids=true | all-gather | bytes 691200 | tf_op jit(solution)/shard_map/all_gather | solution.py:77
  213.9 112.1 %while.30 = (s32[]{:T(128)}, bf16[20,768,64]{1,2,0:T(8,128)(2,1)S(1)}, f32[20,768]{1,0:T(8,128)S(1)}, bf16[20,768,64]{2,1,0:T(8,128)(2,1)}, bf16[20,1024,64]{2,1...) while((s32[]{:T(128)}, bf16[20,768,64]{1,2,0:T(8,128)(2,1)S(1)}, ...), condition=%wide.region_4.5_spmd.clone.clone, body=%wide.region_1.4_spmd.clone.sunk.clone | while | flops 213122304 | bytes 10405977 | solution.py:163
  355.2 31.7 %all-gather.22.cloned.1.call-done = bf16[960,2560]{0,1:T(8,128)(2,1)} async-done(((bf16[960,320]{0,1:T(8,128)(2,1)}), bf16[960,2560]{0,1:T(8,128)(2,1)}) %all-gather.22.cloned.1.call-update) | async-done | bytes 4915216 | tf_op jit(solution)/shard_map/all_gather | solution.py:79
  397.9 71.2 %all-gather.26.cloned.1.call-done = bf16[2560,960]{0,1:T(8,128)(2,1)} async-done(((bf16[2560,120]{0,1:T(8,128)(2,1)}), bf16[2560,960]{0,1:T(8,128)(2,1)}) %all-gather.26.cloned.1.call-update) | async-done | bytes 4915216 | tf_op jit(solution)/shard_map/all_gather | solution.py:191
  469.1 19.1 multiply_convert_fusion.1
  524.2 220.3 %while.31 = (s32[]{:T(128)}, f32[20,768,64]{1,2,0:T(8,128)}, f32[20,1024,64]{1,2,0:T(8,128)}, f32[20,1024,64]{1,2,0:T(8,128)}, bf16[20,768,64]{2,1,0:T(8,128)(2,...) while((s32[]{:T(128)}, f32[20,768,64]{1,2,0:T(8,128)}, ...), condition=%wide.region_9.10_spmd.clone.clone, body=%wide.region_7.9_spmd.clone.sunk.clone | while | flops 511294720 | bytes 25910384 | solution.py:262
  753.5 77.4 %copy.93 = f32[4,1024,320]{0,2,1:T(8,128)} copy(f32[4,1024,320]{1,0,2:T(4,128)} %bitcast.268) | data formatting | bytes 10485760
  830.9 144.6 %reshape.360 = f32[1024,1280]{1,0:T(8,128)} reshape(f32[1024,320,4]{2,1,0:T(8,128)} %bitcast.50) | data formatting | bytes 10485760
  1025.1 47.0 %reshape.361 = bf16[256,320,4]{2,1,0:T(8,128)(2,1)} reshape(f32[256,1280]{1,0:T(8,128)} %reduce-scatter.53.cloned.1.call-done) | data formatting | bytes 1966080
  1135.2 24.9 %collective-permute-done = bf16[2560,120]{0,1:T(8,128)(2,1)S(1)} collective-permute-done((bf16[2560,120]{0,1:T(8,128)(2,1)S(1)}, bf16[2560,120]{0,1:T(8,128)(2,1)S(1)}, u32[]{:S(2)}, u32[]{:S(2)}) %collective-permute-start) | collective-permute-done | bytes 614432 | tf_op jit(solution)/shard_map/ppermute | solution.py:22
  1168.2 71.2 %reduce-scatter.57.cloned.1.call-done = f32[120,960]{1,0:T(8,128)} async-done(((f32[960,960]{1,0:T(8,128)}), f32[120,960]{1,0:T(8,128)}) %reduce-scatter.57.cloned.1.call-update) | async-done | bytes 460816
  1251.2 56.1 %reduce-scatter.39.cloned.1.call-done = f32[960,40]{0,1:T(8,128)} async-done(((f32[960,320]{0,1:T(8,128)}), f32[960,40]{0,1:T(8,128)}) %reduce-scatter.39.cloned.1.call-update) | async-done | bytes 153616 | tf_op jit(solution)/shard_map/reduce_scatter | solution.py:313
  1309.3 65.4 %reduce-scatter.41.cloned.1.call-done = f32[960,40]{0,1:T(8,128)} async-done(((f32[960,320]{0,1:T(8,128)}), f32[960,40]{0,1:T(8,128)}) %reduce-scatter.41.cloned.1.call-update) | async-done | bytes 153616 | tf_op jit(solution)/shard_map/reduce_scatter | solution.py:314
  1376.7 178.6 %reduce-scatter.47.cloned.1.call-done = f32[960,320]{0,1:T(8,128)} async-done(((f32[960,2560]{0,1:T(8,128)}), f32[960,320]{0,1:T(8,128)}) %reduce-scatter.47.cloned.1.call-update) | async-done | bytes 1228816 | tf_op jit(solution)/shard_map/reduce_scatter | solution.py:317
  1563.0 263.7 %reduce-scatter.45.cloned.1.call-done = f32[960,320]{0,1:T(8,128)} async-done(((f32[960,2560]{0,1:T(8,128)}), f32[960,320]{0,1:T(8,128)}) %reduce-scatter.45.cloned.1.call-update) | async-done | bytes 1228816 | tf_op jit(solution)/shard_map/reduce_scatter | solution.py:316
  1841.2 157.9 %reduce-scatter.49.cloned.1.call-done = f32[2560,120]{0,1:T(8,128)} async-done(((f32[2560,960]{0,1:T(8,128)}), f32[2560,120]{0,1:T(8,128)}) %reduce-scatter.49.cloned.1.call-update) | async-done | bytes 1228816 | tf_op jit(solution)/shard_map/reduce_scatter | solution.py:318
  2023.4 22.2 reduce-scatter.37.cloned.1.call-done
  2054.0 59.1 %reduce-scatter.55.cloned.1.call-done = f32[240,1]{1,0:T(8,128)} async-done(((f32[1920,1]{1,0:T(8,128)}), f32[240,1]{1,0:T(8,128)}) %reduce-scatter.55.cloned.1.call-update) | async-done | bytes 976
  2136.8 23.0 %reduce-scatter.61.cloned.1.call-done = f32[240,40]{1,0:T(8,128)} async-done(((f32[960,40]{1,0:T(8,128)}), f32[240,40]{1,0:T(8,128)}) %reduce-scatter.61.cloned.1.call-update) | async-done | bytes 38416
  2162.0 27.8 %reduce-scatter.67.cloned.1.call-done = f32[240,320]{1,0:T(8,128)} async-done(((f32[960,320]{1,0:T(8,128)}), f32[240,320]{1,0:T(8,128)}) %reduce-scatter.67.cloned.1.call-update) | async-done | bytes 307216
  2190.9 28.9 %reduce-scatter.65.cloned.1.call-done = f32[240,320]{1,0:T(8,128)} async-done(((f32[960,320]{1,0:T(8,128)}), f32[240,320]{1,0:T(8,128)}) %reduce-scatter.65.cloned.1.call-update) | async-done | bytes 307216
  2222.5 25.7 %reduce-scatter.51.cloned.1.call-done = f32[640,120]{0,1:T(8,128)} async-done(((f32[2560,120]{0,1:T(8,128)}), f32[640,120]{0,1:T(8,128)}) %reduce-scatter.51.cloned.1.call-update) | async-done | bytes 307216 | tf_op jit(solution)/shard_map/reduce_scatter | solution.py:328
  (559 shorter events, 756.4 us)
Async XLA Ops:
  7.2 170.8 %all-gather.14.cloned.1.call-start = ((), (), s32[]{:S(2)}) async-start(), calls=%async_computation.17 | async-start | bytes 2211840 | tf_op jit(solution)/shard_map/all_gather | solution.py:75
  15.6 171.3 %all-gather.16.cloned.1.call-start = ((), (), s32[]{:S(2)}) async-start(), calls=%async_computation.18 | async-start | bytes 3276800 | tf_op jit(solution)/shard_map/all_gather | solution.py:159
  134.1 200.9 %all-gather.20.cloned.1.call-start = ((), (), s32[]{:S(2)}) async-start(), calls=%async_computation.20 | async-start | bytes 2211840 | tf_op jit(solution)/shard_map/all_gather | solution.py:78
  140.7 202.2 %all-gather.24.cloned.1.call-start = ((), (), s32[]{:S(2)}) async-start(), calls=%async_computation.22 | async-start | bytes 5898240 | tf_op jit(solution)/shard_map/all_gather | solution.py:80
  154.9 232.0 %all-gather.22.cloned.1.call-start = ((), (), s32[]{:S(2)}) async-start(), calls=%async_computation.21 | async-start | bytes 5898240 | tf_op jit(solution)/shard_map/all_gather | solution.py:79
  164.9 304.2 %all-gather.26.cloned.1.call-start = ((), (), s32[]{:S(2)}) async-start(), calls=%async_computation.23 | async-start | bytes 5529600 | tf_op jit(solution)/shard_map/all_gather | solution.py:191
  173.2 834.9 %reduce-scatter.35.cloned.1.call-start = ((), (), s32[]{:S(2)}) async-start(), calls=%async_computation.24 | async-start | bytes 6553600 | tf_op jit(solution)/shard_map/reduce_scatter | solution.py:273
  744.5 280.5 %reduce-scatter.53.cloned.1.call-start = ((), (), s32[]{:S(2)}) async-start(), calls=%async_computation.33 | async-start | bytes 6553600
  983.9 255.5 %reduce-scatter.57.cloned.1.call-start = ((), (), s32[]{:S(2)}) async-start(), calls=%async_computation.35 | async-start | bytes 4423680
  1008.0 299.3 %reduce-scatter.39.cloned.1.call-start = ((), (), s32[]{:S(2)}) async-start(), calls=%async_computation.26 | async-start | bytes 1474560 | tf_op jit(solution)/shard_map/reduce_scatter | solution.py:313
  1013.6 361.1 %reduce-scatter.41.cloned.1.call-start = ((), (), s32[]{:S(2)}) async-start(), calls=%async_computation.27 | async-start | bytes 1474560 | tf_op jit(solution)/shard_map/reduce_scatter | solution.py:314
  1092.9 462.4 %reduce-scatter.47.cloned.1.call-start = ((), (), s32[]{:S(2)}) async-start(), calls=%async_computation.30 | async-start | bytes 11796480 | tf_op jit(solution)/shard_map/reduce_scatter | solution.py:317
  1103.8 722.9 %reduce-scatter.45.cloned.1.call-start = ((), (), s32[]{:S(2)}) async-start(), calls=%async_computation.29 | async-start | bytes 11796480 | tf_op jit(solution)/shard_map/reduce_scatter | solution.py:316
  1116.1 882.9 %reduce-scatter.49.cloned.1.call-start = ((), (), s32[]{:S(2)}) async-start(), calls=%async_computation.31 | async-start | bytes 11059200 | tf_op jit(solution)/shard_map/reduce_scatter | solution.py:318
  1127.9 894.0 %reduce-scatter.43.cloned.1.call-start = ((), (), s32[]{:S(2)}) async-start(), calls=%async_computation.28 | async-start | bytes 614400 | tf_op jit(solution)/shard_map/reduce_scatter | solution.py:325
  1135.2 910.4 %reduce-scatter.37.cloned.1.call-start = ((), (), s32[]{:S(2)}) async-start(), calls=%async_computation.25 | async-start | bytes 614400 | tf_op jit(solution)/shard_map/reduce_scatter | solution.py:322
  1161.2 397.0 %collective-permute-start.1 = (bf16[2560,240]{0,1:T(8,128)(2,1)}, bf16[2560,240]{0,1:T(8,128)(2,1)S(1)}, u32[]{:S(2)}, u32[]{:S(2)}) collective-permute-start(bf16[2560,240]{0,1:T(8,128)(2,1)} %pad_maximum_fusion.1), channel_id=1, source_target_pairs={{0,24},{4,28},{8,0},{12,4},{16,8},{20,12},{24,16},{28,20},{1,25},{... | collective-permute-start | bytes 3686408 | tf_op jit(solution)/shard_map/ppermute | solution.py:22
  1241.5 871.6 %reduce-scatter.55.cloned.1.call-start = ((), (), s32[]{:S(2)}) async-start(), calls=%async_computation.34 | async-start | bytes 1105920
  1251.1 884.7 %reduce-scatter.59.cloned.1.call-start = ((), (), s32[]{:S(2)}) async-start(), calls=%async_computation.36 | async-start | bytes 614400
  1309.2 850.5 %reduce-scatter.61.cloned.1.call-start = ((), (), s32[]{:S(2)}) async-start(), calls=%async_computation.37 | async-start | bytes 614400
  1376.6 813.1 %reduce-scatter.67.cloned.1.call-start = ((), (), s32[]{:S(2)}) async-start(), calls=%async_computation.40 | async-start | bytes 1843200
  1558.2 661.6 %reduce-scatter.65.cloned.1.call-start = ((), (), s32[]{:S(2)}) async-start(), calls=%async_computation.39 | async-start | bytes 1843200
  1559.9 271.8 %collective-permute-start.2 = (bf16[2560,480]{0,1:T(8,128)(2,1)}, bf16[2560,480]{0,1:T(8,128)(2,1)}, u32[]{:S(2)}, u32[]{:S(2)}) collective-permute-start(bf16[2560,480]{0,1:T(8,128)(2,1)} %pad_maximum_fusion), channel_id=1, source_target_pairs={{0,16},{4,20},{8,24},{12,28},{16,0},{20,4},{24,8},{28,12},{1,17},{... | collective-permute-start | bytes 7372808 | tf_op jit(solution)/shard_map/ppermute | solution.py:22
  1829.6 418.6 %reduce-scatter.51.cloned.1.call-start = ((), (), s32[]{:S(2)}) async-start(), calls=%async_computation.32 | async-start | bytes 1536000 | tf_op jit(solution)/shard_map/reduce_scatter | solution.py:328
  (49 other events, 1294.6 us)
Sparse Core Ops, SparseCore 0:
  15.7 49.7 all-gather.13
  92.7 22.3 all-gather.15
  134.2 25.9 all-gather.17
  162.8 51.2 all-gather.19
  216.1 84.4 all-gather.23
  302.6 84.2 all-gather.21
  389.1 79.9 all-gather.25
  744.7 49.4 reduce-scatter.34
  975.6 49.4 reduce-scatter.52
  1028.6 84.5 reduce-scatter.62
  1116.8 122.5 reduce-scatter.56
  1242.7 64.6 reduce-scatter.38
  1310.7 63.9 reduce-scatter.40
  1378.1 177.1 reduce-scatter.46
  1558.8 267.8 reduce-scatter.44
  1830.2 168.8 reduce-scatter.48
  2001.4 20.3 reduce-scatter.42
  2024.2 21.3 reduce-scatter.36
  2049.0 64.0 reduce-scatter.54
  2115.4 20.3 reduce-scatter.58
  2138.3 21.3 reduce-scatter.60
  2162.3 27.3 reduce-scatter.66
  2192.3 27.4 reduce-scatter.64
  2222.3 25.9 reduce-scatter.50
